TPU v7x, 32 devices: a whole 2x2x4 slice. The times are simulated.
32 devices in a mesh: tok: 8 (over y, x, core), mdl: 4 (over z).
Axes of the slice: x: 2, y: 2, z: 4, core: 2. Of those that a mesh axis runs over, the one named last changes fastest.
Arguments:
- hidden_states: bfloat16 [4096, 3072], P('tok', 'mdl'), may hold values from -36 to 36
- lengths: int32 [2], replicated, may hold values from 1 to 2277, 3644 in all
- positions: int32 [3, 4096], P(None, 'tok'), may hold values from 0 to 44, as said below
- modulation: float32 [6, 3072], replicated, may hold values from -3 to 3
- query_weight: bfloat16 [3072, 3072], P('tok', 'mdl'), may hold values from -1.1 to 1.1
- key_weight: bfloat16 [3072, 3072], P('tok', 'mdl'), may hold values from -1.1 to 1.1
- value_weight: bfloat16 [3072, 3072], P('tok', 'mdl'), may hold values from -0.109375 to 0.109375
- out_weight: bfloat16 [3072, 3072], P('tok', 'mdl'), may hold values from -0.109375 to 0.109375
- query_gain: float32 [64], replicated, may hold values from 0.1 to 1.9
- key_gain: float32 [64], replicated, may hold values from 0.1 to 1.9
Outputs:
- updated: bfloat16 [4096, 3072], P('tok', 'mdl')
Inputs may be any that keep to these rules, and one draw needn't show every extreme that they name: lengths[0] + lengths[1] = 3644, and neither of them exceeds 2277. `positions`: frame below 13, row below 30, column below 45.
All inputs are finite; a program needn't handle non-finite values.
Results may differ from a plain program's by a relative error of at most 0.0045.
Values may be sent and summed in bfloat16 or wider, within the bound.
A program may use at most 128 MiB of HBM per device.

v0:
```python
import jax
import jax.numpy as jnp
from jax import lax
from jax.sharding import PartitionSpec as P

TEXT = 226


def token_labels(row_index, lengths):
    bound = TEXT + lengths[0]
    request = (row_index >= bound).astype(jnp.int32)
    place = row_index - request * bound
    return (request, place < TEXT, bound)


def modulate(rows_bf, modulation, is_text):
    values = rows_bf.astype(jnp.float32)
    center = values - jnp.mean(values, axis=1, keepdims=True)
    spread = jnp.mean(center * center, axis=1, keepdims=True)
    normal = center * lax.rsqrt(spread + 1e-05)
    textual = is_text[:, None]
    shift = jnp.where(textual, modulation[3][None, :], modulation[0][None, :])
    scale = jnp.where(textual, modulation[4][None, :], modulation[1][None, :])
    return (normal * (1.0 + scale) + shift).astype(jnp.bfloat16)


def pair_angles(positions, pairs):
    index = jnp.arange(pairs, dtype=jnp.int32)
    first = pairs // 4
    second = (pairs - first) // 2
    third = pairs - first - second
    component = jnp.where(index < first, 0, jnp.where(index < first + second, 1, 2))
    local = index - jnp.where(component == 0, 0, jnp.where(component == 1, first, first + second))
    count = jnp.where(component == 0, first, jnp.where(component == 1, second, third))
    rates = jnp.power(jnp.float32(10000.0), -local.astype(jnp.float32) / count.astype(jnp.float32))
    places = positions.astype(jnp.float32)
    chosen = jnp.where(
        component[:, None] == 0,
        places[0][None, :],
        jnp.where(component[:, None] == 1, places[1][None, :], places[2][None, :]),
    )
    return jnp.transpose(chosen * rates[:, None])


def head_norm(projected, gain, angles, is_text):
    width = gain.shape[0]
    shaped = projected.reshape(projected.shape[0], -1, width)
    center = shaped - jnp.mean(shaped, axis=2, keepdims=True)
    spread = jnp.mean(center * center, axis=2, keepdims=True)
    normal = center * lax.rsqrt(spread + 1e-06) * gain
    half = width // 2
    cosine = jnp.cos(angles)[:, None, :]
    sine = jnp.sin(angles)[:, None, :]
    lower = normal[:, :, :half]
    upper = normal[:, :, half:]
    turned = jnp.concatenate([lower * cosine - upper * sine, lower * sine + upper * cosine], axis=2)
    return jnp.where(is_text[:, None, None], normal, turned).astype(jnp.bfloat16)


def shards(
    hidden_states,
    lengths,
    positions,
    modulation,
    query_weight,
    key_weight,
    value_weight,
    out_weight,
    query_gain,
    key_gain,
):
    own_rows = hidden_states.shape[0]
    local_width = query_weight.shape[1]
    head_width = query_gain.shape[0]
    local_heads = local_width // head_width
    full_rows = lax.all_gather(hidden_states, "mdl", axis=1, tiled=True)
    row_index = lax.axis_index("tok") * own_rows + jnp.arange(own_rows, dtype=jnp.int32)
    request, is_text, bound = token_labels(row_index, lengths)
    normed = modulate(full_rows, modulation, is_text)
    angles = pair_angles(positions, head_width // 2)
    pieces = (
        lax.all_gather(query_weight, "tok", axis=0, tiled=True),
        lax.all_gather(key_weight, "tok", axis=0, tiled=True),
        lax.all_gather(value_weight, "tok", axis=0, tiled=True),
    )
    columns = normed
    query_sum, key_sum, value_sum = tuple(
        (
            jnp.dot(columns, pieces[number], preferred_element_type=jnp.float32)
            for number in range(3)
        )
    )
    query = head_norm(query_sum, query_gain, angles, is_text)
    key_flat = head_norm(key_sum, key_gain, angles, is_text).reshape(own_rows, local_width)
    value_flat = value_sum.astype(jnp.bfloat16)
    factor = head_width ** (-0.5)

    def block_terms(block_keys, block_values, block_start):
        size = block_keys.shape[0]
        key_request = (block_start + jnp.arange(size, dtype=jnp.int32) >= bound).astype(jnp.int32)
        score = (
            jnp.einsum(
                "qhd,khd->hqk",
                query,
                block_keys.reshape(size, local_heads, head_width),
                preferred_element_type=jnp.float32,
            )
            * factor
        )
        same = (request[:, None] == key_request[None, :])[None, :, :]
        expo = jnp.where(same, jnp.exp(score), jnp.float32(0.0))
        totals = jnp.transpose(jnp.sum(expo, axis=2))
        weighted = jnp.einsum(
            "hqk,khd->qhd",
            expo.astype(jnp.bfloat16),
            block_values.reshape(size, local_heads, head_width),
            preferred_element_type=jnp.float32,
        )
        return (weighted.reshape(own_rows, local_width), totals)

    initial = (
        jnp.zeros((own_rows, local_width), jnp.float32),
        jnp.zeros((own_rows, local_heads), jnp.float32),
    )
    keys_piece = lax.all_gather(key_flat, "tok", axis=0, tiled=True)
    values_piece = lax.all_gather(value_flat, "tok", axis=0, tiled=True)
    count = keys_piece.shape[0]
    block = 1024
    steps_count = count // block

    def step_block(inner, operands):
        block_keys, block_values, offset = operands
        weighted, totals = block_terms(block_keys, block_values, offset)
        return ((inner[0] + weighted, inner[1] + totals), None)

    offsets = jnp.arange(steps_count, dtype=jnp.int32) * block
    result, unused = lax.scan(
        step_block,
        initial,
        (
            keys_piece.reshape(steps_count, block, local_width),
            values_piece.reshape(steps_count, block, local_width),
            offsets,
        ),
    )
    weighted, totals = result
    attended = (
        (weighted.reshape(own_rows, local_heads, head_width) / totals[:, :, None])
        .reshape(own_rows, local_width)
        .astype(jnp.bfloat16)
    )
    all_heads = lax.all_gather(attended, "mdl", axis=1, tiled=True)
    out_width = out_weight.shape[1]
    columns = all_heads
    projected = jnp.dot(
        columns,
        lax.all_gather(out_weight, "tok", axis=0, tiled=True),
        preferred_element_type=jnp.float32,
    )
    gate_rows = lax.dynamic_slice_in_dim(
        modulation, lax.axis_index("mdl") * out_width, out_width, 1
    )
    gate = jnp.where(is_text[:, None], gate_rows[5][None, :], gate_rows[2][None, :])
    return (hidden_states.astype(jnp.float32) + gate * projected).astype(jnp.bfloat16)


def solution(mesh):
    return jax.shard_map(
        shards,
        mesh=mesh,
        in_specs=(
            P("tok", "mdl"),
            P(),
            P(None, "tok"),
            P(),
            P("tok", "mdl"),
            P("tok", "mdl"),
            P("tok", "mdl"),
            P("tok", "mdl"),
            P(),
            P(),
        ),
        out_specs=P("tok", "mdl"),
        check_vma=False,
    )
```

profile of v0, /device:TPU:0, one launch (start us, length us, event | category | flops | bytes accessed | tf_op | source)
XLA Modules:
  0.0 505.0 jit_solution(1737966056882740450)
XLA Ops:
  10.6 64.5 %all-gather.9.cloned.1.call-done = bf16[512,3072]{1,0:T(8,128)(2,1)} async-done(((bf16[512,768]{1,0:T(8,128)(2,1)}), bf16[512,3072]{1,0:T(8,128)(2,1)}) %all-gather.9.cloned.1.call-update) | async-done | bytes 3145744 | tf_op jit(solution)/shard_map/all_gather | solution.py:76
  75.1 2.5 convert_reduce_fusion
  78.9 3.7 fusion.16
  82.7 32.0 %all-gather.15.cloned.1.call-done = bf16[3072,768]{1,0:T(8,128)(2,1)} async-done(((bf16[384,768]{1,0:T(8,128)(2,1)}), bf16[3072,768]{1,0:T(8,128)(2,1)}) %all-gather.15.cloned.1.call-update) | async-done | bytes 4718608 | tf_op jit(solution)/shard_map/all_gather | solution.py:83
  114.7 5.9 %fusion.25 = f32[512,768]{1,0:T(8,128)S(1)} fusion(bf16[512,3072]{1,0:T(8,128)(2,1)} %fusion.16, bf16[3072,768]{1,0:T(8,128)(2,1)} %all-gather.15.cloned.1.call-done), kind=kOutput, calls=%fused_computation.64 | convolution fusion | flops 2415919104 | bytes 9437184 | tf_op jit(solution)/shard_map/dot_general | solution.py:89
  121.9 33.6 %all-gather.19.cloned.1.call-done = bf16[3072,768]{1,0:T(8,128)(2,1)} async-done(((bf16[384,768]{1,0:T(8,128)(2,1)}), bf16[3072,768]{1,0:T(8,128)(2,1)}) %all-gather.19.cloned.1.call-update) | async-done | bytes 4718608 | tf_op jit(solution)/shard_map/all_gather | solution.py:82
  155.5 5.5 %fusion.26 = f32[512,768]{0,1:T(8,128)S(1)} fusion(bf16[512,3072]{1,0:T(8,128)(2,1)} %fusion.16, bf16[3072,768]{1,0:T(8,128)(2,1)} %all-gather.19.cloned.1.call-done), kind=kOutput, calls=%fused_computation.65 | convolution fusion | flops 2415919104 | bytes 9437184 | tf_op jit(solution)/shard_map/dot_general | solution.py:89
  166.9 1.7 copy.22
  169.5 1.6 copy.21
  171.1 3.8 select_convert_fusion
  175.1 21.0 %all-gather.11.cloned.1.call-done = bf16[3072,768]{1,0:T(8,128)(2,1)} async-done(((bf16[384,768]{1,0:T(8,128)(2,1)}), bf16[3072,768]{1,0:T(8,128)(2,1)}) %all-gather.11.cloned.1.call-update) | async-done | bytes 4718608 | tf_op jit(solution)/shard_map/all_gather | solution.py:84
  196.2 6.8 %convolution_convert_fusion = bf16[512,768]{1,0:T(8,128)(2,1)} fusion(bf16[512,3072]{1,0:T(8,128)(2,1)} %fusion.16, bf16[3072,768]{1,0:T(8,128)(2,1)} %all-gather.11.cloned.1.call-done), kind=kOutput, calls=%fused_computation.36 | convolution fusion | flops 2416312320 | bytes 8650752 | tf_op jit(solution)/shard_map/dot_general | solution.py:89
  205.3 38.2 %all-gather.17.cloned.1.call-done = bf16[4096,768]{1,0:T(8,128)(2,1)} async-done(((bf16[512,768]{1,0:T(8,128)(2,1)}), bf16[4096,768]{1,0:T(8,128)(2,1)}) %all-gather.17.cloned.1.call-update) | async-done | bytes 6291472 | tf_op jit(solution)/shard_map/all_gather | solution.py:125
  243.5 47.3 %all-gather.13.cloned.1.call-done = bf16[4096,768]{1,0:T(8,128)(2,1)} async-done(((bf16[512,768]{1,0:T(8,128)(2,1)}), bf16[4096,768]{1,0:T(8,128)(2,1)}) %all-gather.13.cloned.1.call-update) | async-done | bytes 6291472 | tf_op jit(solution)/shard_map/all_gather | solution.py:126
  290.8 134.3 %while.15 = (s32[]{:T(128)}, f32[512,768]{0,1:T(8,128)}, f32[512,12]{0,1:T(8,128)}, bf16[4,1024,768]{2,1,0:T(8,128)(2,1)}, s32[4]{0:T(128)S(1)}, /*index=5*/s32[...) while((s32[]{:T(128)}, f32[512,768]{0,1:T(8,128)}, ...), condition=%wide.region_8.9_spmd.clone.clone.clone, body=%wide.region_6.8_spmd.clone.clone.clone.sunk | while | flops 1649682944 | bytes 87601416 | solution.py:137
  293.2 2.1 constant_dynamic-slice_fusion.3
  295.3 1.6 copy.34
  296.9 13.0 %fusion.52 = (f32[12,512]{1,0:T(8,128)S(1)}, f32[12,1024,512]{2,1,0:T(8,128)}) fusion(pred[512,1024]{0,1:T(8,128)(4,1)} %broadcast_compare_fusion.4, bf16[1024,12,64]{0,2,1:T(8,128)(2,1)} %bitcast.67, bf16[512,12,64]{0,2,1:T(8,128)(2,1)} %get-tuple-element.289), kind=kOutput, calls=%fused_computation.2.clone.1 | convolution fusion | flops 824174592 | bytes 28073984 | tf_op jit(solution)/shard_map/while/body/eval_jaxpr/qhd,khd->hqk/dot_general | solution.py:102
  311.5 11.7 %fusion.53 = f32[12,64,512]{2,1,0:T(8,128)S(1)} fusion(bf16[1024,12,64]{0,2,1:T(8,128)(2,1)} %bitcast.68, f32[12,1024,512]{2,1,0:T(8,128)} %get-tuple-element.258, pred[512,1024]{0,1:T(8,128)(4,1)} %broadcast_compare_fusion.4), kind=kOutput, calls=%fused_computation.4.clone.1 | convolution fusion | flops 824180736 | bytes 28835840 | tf_op jit(solution)/shard_map/while/body/eval_jaxpr/hqk,khd->qhd/dot_general | solution.py:113
  327.3 2.1 constant_dynamic-slice_fusion.3
  331.1 13.0 %fusion.52 = (f32[12,512]{1,0:T(8,128)S(1)}, f32[12,1024,512]{2,1,0:T(8,128)}) fusion(pred[512,1024]{0,1:T(8,128)(4,1)} %broadcast_compare_fusion.4, bf16[1024,12,64]{0,2,1:T(8,128)(2,1)} %bitcast.67, bf16[512,12,64]{0,2,1:T(8,128)(2,1)} %get-tuple-element.289), kind=kOutput, calls=%fused_computation.2.clone.1 | convolution fusion | flops 824174592 | bytes 28073984 | tf_op jit(solution)/shard_map/while/body/eval_jaxpr/qhd,khd->hqk/dot_general | solution.py:102
  345.7 10.9 %fusion.53 = f32[12,64,512]{2,1,0:T(8,128)S(1)} fusion(bf16[1024,12,64]{0,2,1:T(8,128)(2,1)} %bitcast.68, f32[12,1024,512]{2,1,0:T(8,128)} %get-tuple-element.258, pred[512,1024]{0,1:T(8,128)(4,1)} %broadcast_compare_fusion.4), kind=kOutput, calls=%fused_computation.4.clone.1 | convolution fusion | flops 824180736 | bytes 28835840 | tf_op jit(solution)/shard_map/while/body/eval_jaxpr/hqk,khd->qhd/dot_general | solution.py:113
  360.8 2.1 constant_dynamic-slice_fusion.3
  362.8 1.6 copy.34
  364.5 13.0 %fusion.52 = (f32[12,512]{1,0:T(8,128)S(1)}, f32[12,1024,512]{2,1,0:T(8,128)}) fusion(pred[512,1024]{0,1:T(8,128)(4,1)} %broadcast_compare_fusion.4, bf16[1024,12,64]{0,2,1:T(8,128)(2,1)} %bitcast.67, bf16[512,12,64]{0,2,1:T(8,128)(2,1)} %get-tuple-element.289), kind=kOutput, calls=%fused_computation.2.clone.1 | convolution fusion | flops 824174592 | bytes 28073984 | tf_op jit(solution)/shard_map/while/body/eval_jaxpr/qhd,khd->hqk/dot_general | solution.py:102
  379.1 10.9 %fusion.53 = f32[12,64,512]{2,1,0:T(8,128)S(1)} fusion(bf16[1024,12,64]{0,2,1:T(8,128)(2,1)} %bitcast.68, f32[12,1024,512]{2,1,0:T(8,128)} %get-tuple-element.258, pred[512,1024]{0,1:T(8,128)(4,1)} %broadcast_compare_fusion.4), kind=kOutput, calls=%fused_computation.4.clone.1 | convolution fusion | flops 824180736 | bytes 28835840 | tf_op jit(solution)/shard_map/while/body/eval_jaxpr/hqk,khd->qhd/dot_general | solution.py:113
  394.1 2.1 constant_dynamic-slice_fusion.3
  397.8 13.0 %fusion.52 = (f32[12,512]{1,0:T(8,128)S(1)}, f32[12,1024,512]{2,1,0:T(8,128)}) fusion(pred[512,1024]{0,1:T(8,128)(4,1)} %broadcast_compare_fusion.4, bf16[1024,12,64]{0,2,1:T(8,128)(2,1)} %bitcast.67, bf16[512,12,64]{0,2,1:T(8,128)(2,1)} %get-tuple-element.289), kind=kOutput, calls=%fused_computation.2.clone.1 | convolution fusion | flops 824174592 | bytes 28073984 | tf_op jit(solution)/shard_map/while/body/eval_jaxpr/qhd,khd->hqk/dot_general | solution.py:102
  412.4 10.9 %fusion.53 = f32[12,64,512]{2,1,0:T(8,128)S(1)} fusion(bf16[1024,12,64]{0,2,1:T(8,128)(2,1)} %bitcast.68, f32[12,1024,512]{2,1,0:T(8,128)} %get-tuple-element.258, pred[512,1024]{0,1:T(8,128)(4,1)} %broadcast_compare_fusion.4), kind=kOutput, calls=%fused_computation.4.clone.1 | convolution fusion | flops 824180736 | bytes 28835840 | tf_op jit(solution)/shard_map/while/body/eval_jaxpr/hqk,khd->qhd/dot_general | solution.py:113
  425.0 2.5 fusion.18
  428.6 62.7 %all-gather.21.cloned.1.call-done = bf16[512,3072]{0,1:T(8,128)(2,1)} async-done(((bf16[512,768]{0,1:T(8,128)(2,1)}), bf16[512,3072]{0,1:T(8,128)(2,1)}) %all-gather.21.cloned.1.call-update) | async-done | bytes 3145744 | tf_op jit(solution)/shard_map/all_gather | solution.py:152
  491.3 6.9 %add_convert_fusion = bf16[512,768]{1,0:T(8,128)(2,1)} fusion(bf16[512,768]{1,0:T(8,128)(2,1)S(1)} %copy-done.7, bf16[512,3072]{0,1:T(8,128)(2,1)} %all-gather.21.cloned.1.call-done, bf16[3072,768]{1,0:T(8,128)(2,1)} %all-gather.23.cloned.1.call-done, f32[768]{0:T(1024)S(1)} %get-tuple-element.157, f32[768]{0:T(1024)S(1)} %get-tuple-element.156, ...), kind=kOutput, calls=%fused_computation.30 | convolution fusion | flops 2417885184 | bytes 9443840 | tf_op jit(solution)/shard_map/dot_general | solution.py:155
  (150 shorter events, 42.6 us)
Async XLA Ops:
  6.5 2.9 copy-start.17
  6.5 2.9 copy-start.21
  6.5 3.0 copy-start.22
  6.5 4.1 copy-start.16
  6.5 68.6 %all-gather.9.cloned.1.call-start = ((), (), s32[]{:S(2)}) async-start(), calls=%async_computation | async-start | bytes 3932160 | tf_op jit(solution)/shard_map/all_gather | solution.py:76
  7.3 107.4 %all-gather.15.cloned.1.call-start = ((), (), s32[]{:S(2)}) async-start(), calls=%async_computation.3 | async-start | bytes 5308416 | tf_op jit(solution)/shard_map/all_gather | solution.py:83
  8.0 147.5 %all-gather.19.cloned.1.call-start = ((), (), s32[]{:S(2)}) async-start(), calls=%async_computation.5 | async-start | bytes 5308416 | tf_op jit(solution)/shard_map/all_gather | solution.py:82
  8.8 187.4 %all-gather.11.cloned.1.call-start = ((), (), s32[]{:S(2)}) async-start(), calls=%async_computation.1 | async-start | bytes 5308416 | tf_op jit(solution)/shard_map/all_gather | solution.py:84
  9.3 234.1 %all-gather.17.cloned.1.call-start = ((), (), s32[]{:S(2)}) async-start(), calls=%async_computation.4 | async-start | bytes 7077888 | tf_op jit(solution)/shard_map/all_gather | solution.py:125
  9.6 194.2 %copy-start.18 = (pred[512]{0:T(512)(128)(4,1)}, pred[512]{0:T(512)(128)(4,1)S(1)}, u32[]{:S(2)}) copy-start(pred[512]{0:T(512)(128)(4,1)S(1)} %subtract_compare_fusion) | copy-start | bytes 1540
  75.1 2.8 copy-start.2
  120.6 1.1 copy-start.3
  174.9 28.9 %copy-start.9 = (f32[512,12]{0,1:T(8,128)S(1)}, f32[512,12]{0,1:T(8,128)}, u32[]{:S(2)}) copy-start(f32[512,12]{0,1:T(8,128)} %copy-done.8) | copy-start | bytes 73732
  174.9 28.9 %copy-start.12 = (f32[512,12]{0,1:T(8,128)S(1)}, f32[512,12]{0,1:T(8,128)}, u32[]{:S(2)}) copy-start(f32[512,12]{0,1:T(8,128)} %copy-done.11) | copy-start | bytes 73732
  174.9 115.9 %all-gather.13.cloned.1.call-start = ((), (), s32[]{:S(2)}) async-start(), calls=%async_computation.2 | async-start | bytes 7077888 | tf_op jit(solution)/shard_map/all_gather | solution.py:126
  203.0 1.0 copy-start.4
  203.0 225.6 %all-gather.23.cloned.1.call-start = ((), (), s32[]{:S(2)}) async-start(), calls=%async_computation.7 | async-start | bytes 5308416 | tf_op jit(solution)/shard_map/all_gather | solution.py:157
  203.7 287.5 %all-gather.21.cloned.1.call-start = ((), (), s32[]{:S(2)}) async-start(), calls=%async_computation.6 | async-start | bytes 3932160 | tf_op jit(solution)/shard_map/all_gather | solution.py:152
  311.5 11.7 %copy-start = (f32[512,768]{0,1:T(8,128)S(1)}, f32[512,768]{0,1:T(8,128)}, u32[]{:S(2)}) copy-start(f32[512,768]{0,1:T(8,128)} %get-tuple-element.272) | copy-start | bytes 4718596 | tf_op jit(solution)/shard_map/while
  323.7 1.2 copy-start.1
  324.0 0.9 copy-start.6
  345.7 10.9 %copy-start = (f32[512,768]{0,1:T(8,128)S(1)}, f32[512,768]{0,1:T(8,128)}, u32[]{:S(2)}) copy-start(f32[512,768]{0,1:T(8,128)} %get-tuple-element.272) | copy-start | bytes 4718596 | tf_op jit(solution)/shard_map/while
  357.1 1.2 copy-start.1
  357.4 0.9 copy-start.6
  379.1 10.9 %copy-start = (f32[512,768]{0,1:T(8,128)S(1)}, f32[512,768]{0,1:T(8,128)}, u32[]{:S(2)}) copy-start(f32[512,768]{0,1:T(8,128)} %get-tuple-element.272) | copy-start | bytes 4718596 | tf_op jit(solution)/shard_map/while
  390.5 1.2 copy-start.1
  390.8 0.9 copy-start.6
  412.4 10.9 %copy-start = (f32[512,768]{0,1:T(8,128)S(1)}, f32[512,768]{0,1:T(8,128)}, u32[]{:S(2)}) copy-start(f32[512,768]{0,1:T(8,128)} %get-tuple-element.272) | copy-start | bytes 4718596 | tf_op jit(solution)/shard_map/while
  423.8 1.2 copy-start.1
  424.1 0.9 copy-start.6
  425.0 66.2 %copy-start.7 = (bf16[512,768]{1,0:T(8,128)(2,1)S(1)}, bf16[512,768]{1,0:T(8,128)(2,1)}, u32[]{:S(2)}) copy-start(bf16[512,768]{1,0:T(8,128)(2,1)} %param.12) | copy-start | bytes 2359300
  425.0 66.2 %copy-start.19 = (pred[512]{0:T(512)(128)(4,1)S(1)}, pred[512]{0:T(512)(128)(4,1)}, u32[]{:S(2)}) copy-start(pred[512]{0:T(512)(128)(4,1)} %copy-done.18) | copy-start | bytes 1540
  (11 other events, 7.9 us)
Sparse Core Ops, SparseCore 0:
  8.9 66.1 all-gather.8
  77.0 37.5 all-gather.14
  116.5 38.9 all-gather.18
  157.2 38.9 all-gather.10
  197.9 45.5 all-gather.16
  245.2 45.5 all-gather.12
  292.7 38.9 all-gather.22
  427.7 63.4 all-gather.20
where the time goes:
time: 506 us; the launch traced here: 505 us
  waiting for transfers between devices  303 us (60%)
  matrix products  121 us (24%)
  local copies, waits for them, and re-layouts  38.3 us (8%)
  other arithmetic  28 us (6%)
  between operations  13.9 us (3%)
    all_gather x1, waiting for transfers between devices, shards(): full_rows = lax.all_gather(hidden_states, 'mdl', axis=1, tiled=True)  64.5 us
    all_gather x1, waiting for transfers between devices, shards(): all_heads = lax.all_gather(attended, 'mdl', axis=1, tiled=True)  62.7 us
    dot_general x4, matrix products, block_terms(): jnp.einsum('qhd,khd->hqk', query, block_keys.reshape(size, local_heads, h...  51.9 us
    all_gather x1, waiting for transfers between devices, shards(): values_piece = lax.all_gather(value_flat, 'tok', axis=0, tiled=True)  47.3 us
    dot_general x4, matrix products, block_terms(): jnp.einsum('hqk,khd->qhd', expo.astype(jnp.bfloat16), block_values.reshap...  44.4 us
    all_gather x1, waiting for transfers between devices, shards(): keys_piece = lax.all_gather(key_flat, 'tok', axis=0, tiled=True)  38.2 us
    all_gather x1, waiting for transfers between devices, shards(): lax.all_gather(query_weight, 'tok', axis=0, tiled=True)  33.6 us
    all_gather x1, waiting for transfers between devices, shards(): lax.all_gather(key_weight, 'tok', axis=0, tiled=True)  32 us
  transfers between devices with their start and end apart: 8, of which 7 were waited for; matrix products, arithmetic and copies ran while one was open for 34% of the time, Pallas kernels for 0%

commit v1 on v0

--- a/solution.py
+++ b/solution.py
@@ -4,6 +4,28 @@
 from jax.sharding import PartitionSpec as P
 
 TEXT = 226
+
+
+def in_order(blocks, dim):
+    lengths = list(blocks.shape[1:])
+    lengths[dim] *= blocks.shape[0]
+    return jnp.moveaxis(blocks, 0, dim).reshape(lengths)
+
+
+def ring_gather(x, axis, dim):
+    peers = lax.axis_size(axis)
+    pairs = [(i, (i + 1) % peers) for i in range(peers)]
+    back = [(b, a) for a, b in pairs]
+    lower, upper = ([], [])
+    for step in range(peers - 1):
+        if step % 2 == 0:
+            lower.append(lax.ppermute(lower[-1] if lower else x, axis, pairs))
+        else:
+            upper.append(lax.ppermute(upper[-1] if upper else x, axis, back))
+    blocks = jnp.stack([*lower[::-1], x, *upper])
+    shift = lax.axis_index(axis) - len(lower)
+    blocks = blocks[(jnp.arange(peers) - shift) % peers]
+    return in_order(blocks, dim)
 
 
 def token_labels(row_index, lengths):
@@ -79,7 +101,7 @@
     normed = modulate(full_rows, modulation, is_text)
     angles = pair_angles(positions, head_width // 2)
     pieces = (
-        lax.all_gather(query_weight, "tok", axis=0, tiled=True),
+        ring_gather(query_weight, "tok", 0),
         lax.all_gather(key_weight, "tok", axis=0, tiled=True),
         lax.all_gather(value_weight, "tok", axis=0, tiled=True),
     )

time: 506 us -> 465 us (0.919)
  waiting for transfers between devices: 303 us -> 224 us
  local copies, waits for them, and re-layouts: 38.3 us -> 64.2 us
  starting transfers between devices: 0.49 us -> 8.86 us
    all_gather x1, waiting for transfers between devices: 64.5 us -> 0.01 us  [shards(): full_rows = lax.all_gather(hidden_states, 'mdl', axis=1, tiled=True)]
    ppermute x0 -> x7, waiting for transfers between devices: none -> 34.2 us  [the longest x4 34.2 us: ring_gather(): lower.append(lax.ppermute(lower[-1] if lower else x, axis, pairs))]
    all_gather x1 -> x0, waiting for transfers between devices: 33.6 us -> none  [shards(): lax.all_gather(query_weight, 'tok', axis=0, tiled=True)]
    all_gather x1, waiting for transfers between devices: 32 us -> 21.1 us  [shards(): lax.all_gather(key_weight, 'tok', axis=0, tiled=True)]
    ppermute x0 -> x7, starting transfers between devices: none -> 8.44 us  [the longest x3 7.93 us: ring_gather(): upper.append(lax.ppermute(upper[-1] if upper else x, axis, back))]
    dot_general x1 -> x2, local copies, waits for them, and re-layouts: 0.47 us -> 8.55 us  [shards(): jnp.dot(columns, pieces[number], preferred_element_type=jnp.float32)]
    unnamed x38 -> x53, local copies, waits for them, and re-layouts: 1.93 us -> 9.36 us
    gather x0 -> x1, local copies, waits for them, and re-layouts: none -> 5.45 us  [ring_gather(): blocks = blocks[(jnp.arange(peers) - shift) % peers]]
  transfers between devices with their start and end apart: 8 -> 14, of which waited for: 7 -> 9; matrix products, arithmetic and copies ran while one was open for 34% -> 44% of each run, Pallas kernels for 0% -> 0%
where the time goes in v1:
time: 465 us; the launch traced here: 464 us
  waiting for transfers between devices  224 us (48%)
  matrix products  120 us (26%)
  local copies, waits for them, and re-layouts  64.2 us (14%)
  other arithmetic  32.5 us (7%)
  between operations  14.5 us (3%)
  starting transfers between devices  8.86 us (2%)
    all_gather x1, waiting for transfers between devices, shards(): all_heads = lax.all_gather(attended, 'mdl', axis=1, tiled=True)  62.7 us
    dot_general x4, matrix products, block_terms(): jnp.einsum('qhd,khd->hqk', query, block_keys.reshape(size, local_heads, h...  51.8 us
    all_gather x1, waiting for transfers between devices, shards(): values_piece = lax.all_gather(value_flat, 'tok', axis=0, tiled=True)  47.3 us
    dot_general x4, matrix products, block_terms(): jnp.einsum('hqk,khd->qhd', expo.astype(jnp.bfloat16), block_values.reshap...  44.4 us
    all_gather x1, waiting for transfers between devices, shards(): keys_piece = lax.all_gather(key_flat, 'tok', axis=0, tiled=True)  38.5 us
    ppermute x4, waiting for transfers between devices, ring_gather(): lower.append(lax.ppermute(lower[-1] if lower else x, axis, pairs))  34.2 us
    dynamic_slice x16, local copies, waits for them, and re-layouts, shards(): lax.scan(step_block, initial, (keys_piece.reshape(steps_count, block, loc...  23.6 us
    all_gather x1, waiting for transfers between devices, shards(): lax.all_gather(key_weight, 'tok', axis=0, tiled=True)  21.1 us
  transfers between devices with their start and end apart: 14, of which 9 were waited for; matrix products, arithmetic and copies ran while one was open for 44% of the time, Pallas kernels for 0%

profile of v1, /device:TPU:0, one launch (start us, length us, event | category | flops | bytes accessed | tf_op | source)
XLA Modules:
  0.0 464.0 jit_solution(3265625731233505681)
XLA Ops:
  8.6 10.7 %collective-permute-done = bf16[384,768]{1,0:T(8,128)(2,1)S(1)} collective-permute-done((bf16[384,768]{1,0:T(8,128)(2,1)}, bf16[384,768]{1,0:T(8,128)(2,1)S(1)}, u32[]{:S(2)}, u32[]{:S(2)}) %collective-permute-start) | collective-permute-done | bytes 589856 | tf_op jit(solution)/shard_map/ppermute | solution.py:22
  19.2 2.6 collective-permute-start.4
  23.8 10.0 %collective-permute-done.1 = bf16[384,768]{1,0:T(8,128)(2,1)S(1)} collective-permute-done((bf16[384,768]{1,0:T(8,128)(2,1)S(1)}, bf16[384,768]{1,0:T(8,128)(2,1)S(1)}, u32[]{:S(2)}, u32[]{:S(2)}) %collective-permute-start.1) | collective-permute-done | bytes 589856 | tf_op jit(solution)/shard_map/ppermute | solution.py:22
  35.5 2.6 collective-permute-start.5
  38.2 10.4 %collective-permute-done.2 = bf16[384,768]{1,0:T(8,128)(2,1)S(1)} collective-permute-done((bf16[384,768]{1,0:T(8,128)(2,1)S(1)}, bf16[384,768]{1,0:T(8,128)(2,1)S(1)}, u32[]{:S(2)}, u32[]{:S(2)}) %collective-permute-start.2) | collective-permute-done | bytes 589856 | tf_op jit(solution)/shard_map/ppermute | solution.py:22
  55.4 2.6 collective-permute-start.6
  58.0 3.1 collective-permute-done.3
  69.1 5.5 %gather_fusion = bf16[8,384,768]{2,1,0:T(8,128)(2,1)} fusion(bf16[8,384,768]{2,1,0:T(8,128)(2,1)} %bitcast_dynamic-update-slice_fusion, s32[1024]{0:T(1024)} %pad_clamp_fusion), kind=kCustom, calls=%fused_computation | custom fusion | bytes 9437216 | tf_op jit(solution)/shard_map/gather | solution.py:27
  74.5 6.6 %copy.24 = bf16[768,3072]{1,0:T(8,128)(2,1)} copy(bf16[768,3072]{0,1:T(8,128)(2,1)} %bitcast.97) | data formatting | bytes 9437184 | tf_op jit(solution)/shard_map/dot_general | solution.py:111
  81.2 2.8 convert_reduce_fusion
  85.4 2.6 fusion.16
  88.1 2.6 fusion.29
  93.5 21.1 %all-gather.14.cloned.1.call-done = bf16[3072,768]{1,0:T(8,128)(2,1)} async-done(((bf16[384,768]{1,0:T(8,128)(2,1)}), bf16[3072,768]{1,0:T(8,128)(2,1)}) %all-gather.14.cloned.1.call-update) | async-done | bytes 4718608 | tf_op jit(solution)/shard_map/all_gather | solution.py:105
  114.6 7.0 %fusion.30 = f32[512,768]{1,0:T(8,128)} fusion(bf16[512,3072]{1,0:T(8,128)(2,1)} %copy-done.5, bf16[3072,768]{1,0:T(8,128)(2,1)} %all-gather.14.cloned.1.call-done), kind=kOutput, calls=%fused_computation.83 | convolution fusion | flops 2415919104 | bytes 9437184 | tf_op jit(solution)/shard_map/dot_general | solution.py:111
  133.1 3.8 select_convert_fusion
  137.1 18.4 %all-gather.10.cloned.1.call-done = bf16[3072,768]{1,0:T(8,128)(2,1)} async-done(((bf16[384,768]{1,0:T(8,128)(2,1)}), bf16[3072,768]{1,0:T(8,128)(2,1)}) %all-gather.10.cloned.1.call-update) | async-done | bytes 4718608 | tf_op jit(solution)/shard_map/all_gather | solution.py:106
  155.5 6.8 %convolution_convert_fusion = bf16[512,768]{1,0:T(8,128)(2,1)} fusion(bf16[512,3072]{1,0:T(8,128)(2,1)} %copy-done.5, bf16[3072,768]{1,0:T(8,128)(2,1)} %all-gather.10.cloned.1.call-done), kind=kOutput, calls=%fused_computation.39 | convolution fusion | flops 2416312320 | bytes 8650752 | tf_op jit(solution)/shard_map/dot_general | solution.py:111
  164.3 38.5 %all-gather.16.cloned.1.call-done = bf16[4096,768]{1,0:T(8,128)(2,1)} async-done(((bf16[512,768]{1,0:T(8,128)(2,1)}), bf16[4096,768]{1,0:T(8,128)(2,1)}) %all-gather.16.cloned.1.call-update) | async-done | bytes 6291472 | tf_op jit(solution)/shard_map/all_gather | solution.py:147
  202.8 47.3 %all-gather.12.cloned.1.call-done = bf16[4096,768]{1,0:T(8,128)(2,1)} async-done(((bf16[512,768]{1,0:T(8,128)(2,1)}), bf16[4096,768]{1,0:T(8,128)(2,1)}) %all-gather.12.cloned.1.call-update) | async-done | bytes 6291472 | tf_op jit(solution)/shard_map/all_gather | solution.py:148
  250.1 134.0 %while.15 = (s32[]{:T(128)}, f32[512,768]{0,1:T(8,128)}, f32[512,12]{0,1:T(8,128)}, bf16[4,1024,768]{2,1,0:T(8,128)(2,1)}, s32[4]{0:T(128)S(1)}, /*index=5*/s32[...) while((s32[]{:T(128)}, f32[512,768]{0,1:T(8,128)}, ...), condition=%wide.region_8.9_spmd.clone.clone.clone, body=%wide.region_6.8_spmd.clone.clone.clone.sunk | while | flops 1649682944 | bytes 87601416 | solution.py:159
  256.2 13.0 %fusion.55 = (f32[12,512]{1,0:T(8,128)S(1)}, f32[12,1024,512]{2,1,0:T(8,128)}) fusion(pred[512,1024]{0,1:T(8,128)(4,1)} %broadcast_compare_fusion.4, bf16[1024,12,64]{0,2,1:T(8,128)(2,1)} %bitcast.92, bf16[512,12,64]{0,2,1:T(8,128)(2,1)} %get-tuple-element.291), kind=kOutput, calls=%fused_computation.3.clone.1 | convolution fusion | flops 824174592 | bytes 28073984 | tf_op jit(solution)/shard_map/while/body/eval_jaxpr/qhd,khd->hqk/dot_general | solution.py:124
  270.8 11.7 %fusion.56 = f32[12,64,512]{2,1,0:T(8,128)S(1)} fusion(bf16[1024,12,64]{0,2,1:T(8,128)(2,1)} %bitcast.93, f32[12,1024,512]{2,1,0:T(8,128)} %get-tuple-element.260, pred[512,1024]{0,1:T(8,128)(4,1)} %broadcast_compare_fusion.4), kind=kOutput, calls=%fused_computation.5.clone.1 | convolution fusion | flops 824180736 | bytes 28835840 | tf_op jit(solution)/shard_map/while/body/eval_jaxpr/hqk,khd->qhd/dot_general | solution.py:135
  286.6 2.1 constant_dynamic-slice_fusion.3
  290.3 13.0 %fusion.55 = (f32[12,512]{1,0:T(8,128)S(1)}, f32[12,1024,512]{2,1,0:T(8,128)}) fusion(pred[512,1024]{0,1:T(8,128)(4,1)} %broadcast_compare_fusion.4, bf16[1024,12,64]{0,2,1:T(8,128)(2,1)} %bitcast.92, bf16[512,12,64]{0,2,1:T(8,128)(2,1)} %get-tuple-element.291), kind=kOutput, calls=%fused_computation.3.clone.1 | convolution fusion | flops 824174592 | bytes 28073984 | tf_op jit(solution)/shard_map/while/body/eval_jaxpr/qhd,khd->hqk/dot_general | solution.py:124
  304.9 10.9 %fusion.56 = f32[12,64,512]{2,1,0:T(8,128)S(1)} fusion(bf16[1024,12,64]{0,2,1:T(8,128)(2,1)} %bitcast.93, f32[12,1024,512]{2,1,0:T(8,128)} %get-tuple-element.260, pred[512,1024]{0,1:T(8,128)(4,1)} %broadcast_compare_fusion.4), kind=kOutput, calls=%fused_computation.5.clone.1 | convolution fusion | flops 824180736 | bytes 28835840 | tf_op jit(solution)/shard_map/while/body/eval_jaxpr/hqk,khd->qhd/dot_general | solution.py:135
  323.6 13.0 %fusion.55 = (f32[12,512]{1,0:T(8,128)S(1)}, f32[12,1024,512]{2,1,0:T(8,128)}) fusion(pred[512,1024]{0,1:T(8,128)(4,1)} %broadcast_compare_fusion.4, bf16[1024,12,64]{0,2,1:T(8,128)(2,1)} %bitcast.92, bf16[512,12,64]{0,2,1:T(8,128)(2,1)} %get-tuple-element.291), kind=kOutput, calls=%fused_computation.3.clone.1 | convolution fusion | flops 824174592 | bytes 28073984 | tf_op jit(solution)/shard_map/while/body/eval_jaxpr/qhd,khd->hqk/dot_general | solution.py:124
  338.2 10.9 %fusion.56 = f32[12,64,512]{2,1,0:T(8,128)S(1)} fusion(bf16[1024,12,64]{0,2,1:T(8,128)(2,1)} %bitcast.93, f32[12,1024,512]{2,1,0:T(8,128)} %get-tuple-element.260, pred[512,1024]{0,1:T(8,128)(4,1)} %broadcast_compare_fusion.4), kind=kOutput, calls=%fused_computation.5.clone.1 | convolution fusion | flops 824180736 | bytes 28835840 | tf_op jit(solution)/shard_map/while/body/eval_jaxpr/hqk,khd->qhd/dot_general | solution.py:135
  356.9 13.0 %fusion.55 = (f32[12,512]{1,0:T(8,128)S(1)}, f32[12,1024,512]{2,1,0:T(8,128)}) fusion(pred[512,1024]{0,1:T(8,128)(4,1)} %broadcast_compare_fusion.4, bf16[1024,12,64]{0,2,1:T(8,128)(2,1)} %bitcast.92, bf16[512,12,64]{0,2,1:T(8,128)(2,1)} %get-tuple-element.291), kind=kOutput, calls=%fused_computation.3.clone.1 | convolution fusion | flops 824174592 | bytes 28073984 | tf_op jit(solution)/shard_map/while/body/eval_jaxpr/qhd,khd->hqk/dot_general | solution.py:124
  371.5 10.9 %fusion.56 = f32[12,64,512]{2,1,0:T(8,128)S(1)} fusion(bf16[1024,12,64]{0,2,1:T(8,128)(2,1)} %bitcast.93, f32[12,1024,512]{2,1,0:T(8,128)} %get-tuple-element.260, pred[512,1024]{0,1:T(8,128)(4,1)} %broadcast_compare_fusion.4), kind=kOutput, calls=%fused_computation.5.clone.1 | convolution fusion | flops 824180736 | bytes 28835840 | tf_op jit(solution)/shard_map/while/body/eval_jaxpr/hqk,khd->qhd/dot_general | solution.py:135
  384.1 2.5 fusion.20
  387.6 62.7 %all-gather.18.cloned.1.call-done = bf16[512,3072]{0,1:T(8,128)(2,1)} async-done(((bf16[512,768]{0,1:T(8,128)(2,1)}), bf16[512,3072]{0,1:T(8,128)(2,1)}) %all-gather.18.cloned.1.call-update) | async-done | bytes 3145744 | tf_op jit(solution)/shard_map/all_gather | solution.py:174
  450.3 6.9 %add_convert_fusion = bf16[512,768]{1,0:T(8,128)(2,1)} fusion(bf16[512,768]{1,0:T(8,128)(2,1)S(1)} %copy-done.9, bf16[512,3072]{0,1:T(8,128)(2,1)} %all-gather.18.cloned.1.call-done, bf16[3072,768]{1,0:T(8,128)(2,1)} %all-gather.20.cloned.1.call-done, f32[768]{0:T(1024)S(1)} %get-tuple-element.157, f32[768]{0:T(1024)S(1)} %get-tuple-element.156, ...), kind=kOutput, calls=%fused_computation.33 | convolution fusion | flops 2417885184 | bytes 9443840 | tf_op jit(solution)/shard_map/dot_general | solution.py:177
  (180 shorter events, 73.7 us)
Async XLA Ops:
  6.5 74.6 %all-gather.8.cloned.1.call-start = ((), (), s32[]{:S(2)}) async-start(), calls=%async_computation | async-start | bytes 3932160 | tf_op jit(solution)/shard_map/all_gather | solution.py:98
  7.3 58.3 %copy-start.10 = (bf16[384,768]{1,0:T(8,128)(2,1)S(1)}, bf16[384,768]{1,0:T(8,128)(2,1)}, u32[]{:S(2)}) copy-start(bf16[384,768]{1,0:T(8,128)(2,1)} %param.16) | copy-start | bytes 1769476
  7.3 107.4 %all-gather.14.cloned.1.call-start = ((), (), s32[]{:S(2)}) async-start(), calls=%async_computation.3 | async-start | bytes 5308416 | tf_op jit(solution)/shard_map/all_gather | solution.py:105
  8.0 147.5 %all-gather.10.cloned.1.call-start = ((), (), s32[]{:S(2)}) async-start(), calls=%async_computation.1 | async-start | bytes 5308416 | tf_op jit(solution)/shard_map/all_gather | solution.py:106
  8.1 11.2 %collective-permute-start = (bf16[384,768]{1,0:T(8,128)(2,1)}, bf16[384,768]{1,0:T(8,128)(2,1)S(1)}, u32[]{:S(2)}, u32[]{:S(2)}) collective-permute-start(bf16[384,768]{1,0:T(8,128)(2,1)} %param.16), channel_id=1, source_target_pairs={{0,4},{4,8},{8,12},{12,16},{16,20},{20,24},{24,28},{28,0},{1,5},{5... | collective-permute-start | bytes 1769480 | tf_op jit(solution)/shard_map/ppermute | solution.py:22
  19.2 14.6 %collective-permute-start.1 = (bf16[384,768]{1,0:T(8,128)(2,1)S(1)}, bf16[384,768]{1,0:T(8,128)(2,1)S(1)}, u32[]{:S(2)}, u32[]{:S(2)}) collective-permute-start(bf16[384,768]{1,0:T(8,128)(2,1)S(1)} %collective-permute-done), channel_id=1, source_target_pairs={{0,4},{4,8},{8,12},{12,16},{16,20},{20,24},{24,28},{28,0},{1,5},{5... | collective-permute-start | bytes 1769480 | tf_op jit(solution)/shard_map/ppermute | solution.py:22
  19.2 16.3 %collective-permute-start.4 = (bf16[384,768]{1,0:T(8,128)(2,1)}, bf16[384,768]{1,0:T(8,128)(2,1)S(1)}, u32[]{:S(2)}, u32[]{:S(2)}) collective-permute-start(bf16[384,768]{1,0:T(8,128)(2,1)} %param.16), channel_id=1, source_target_pairs={{4,0},{8,4},{12,8},{16,12},{20,16},{24,20},{28,24},{0,28},{5,1},{9... | collective-permute-start | bytes 1769480 | tf_op jit(solution)/shard_map/ppermute | solution.py:24
  21.9 180.9 %all-gather.16.cloned.1.call-start = ((), (), s32[]{:S(2)}) async-start(), calls=%async_computation.4 | async-start | bytes 7077888 | tf_op jit(solution)/shard_map/all_gather | solution.py:147
  33.8 14.8 %collective-permute-start.2 = (bf16[384,768]{1,0:T(8,128)(2,1)S(1)}, bf16[384,768]{1,0:T(8,128)(2,1)S(1)}, u32[]{:S(2)}, u32[]{:S(2)}) collective-permute-start(bf16[384,768]{1,0:T(8,128)(2,1)S(1)} %collective-permute-done.1), channel_id=1, source_target_pairs={{0,4},{4,8},{8,12},{12,16},{16,20},{20,24},{24,28},{28,0},{1,5},{5... | collective-permute-start | bytes 1769480 | tf_op jit(solution)/shard_map/ppermute | solution.py:22
  35.5 19.9 %collective-permute-start.5 = (bf16[384,768]{1,0:T(8,128)(2,1)S(1)}, bf16[384,768]{1,0:T(8,128)(2,1)S(1)}, u32[]{:S(2)}, u32[]{:S(2)}) collective-permute-start(bf16[384,768]{1,0:T(8,128)(2,1)S(1)} %collective-permute-done.4), channel_id=1, source_target_pairs={{4,0},{8,4},{12,8},{16,12},{20,16},{24,20},{28,24},{0,28},{5,1},{9... | collective-permute-start | bytes 1769480 | tf_op jit(solution)/shard_map/ppermute | solution.py:24
  48.6 12.5 %collective-permute-start.3 = (bf16[384,768]{1,0:T(8,128)(2,1)S(1)}, bf16[384,768]{1,0:T(8,128)(2,1)}, u32[]{:S(2)}, u32[]{:S(2)}) collective-permute-start(bf16[384,768]{1,0:T(8,128)(2,1)S(1)} %collective-permute-done.2), channel_id=1, source_target_pairs={{0,4},{4,8},{8,12},{12,16},{16,20},{20,24},{24,28},{28,0},{1,5},{5... | collective-permute-start | bytes 1769480 | tf_op jit(solution)/shard_map/ppermute | solution.py:22
  55.4 12.8 %collective-permute-start.6 = (bf16[384,768]{1,0:T(8,128)(2,1)S(1)}, bf16[384,768]{1,0:T(8,128)(2,1)S(1)}, u32[]{:S(2)}, u32[]{:S(2)}) collective-permute-start(bf16[384,768]{1,0:T(8,128)(2,1)S(1)} %collective-permute-done.5), channel_id=1, source_target_pairs={{4,0},{8,4},{12,8},{16,12},{20,16},{24,20},{28,24},{0,28},{5,1},{9... | collective-permute-start | bytes 1769480 | tf_op jit(solution)/shard_map/ppermute | solution.py:24
  81.2 4.2 copy-start.22
  81.2 3.3 copy-start.2
  81.2 4.2 copy-start.19
  81.2 4.2 copy-start.20
  81.2 4.2 copy-start.21
  85.4 2.6 copy-start.4
  88.0 2.7 copy-start.5
  88.1 3.9 copy-start.25
  136.9 26.1 %copy-start.6 = (bf16[512,12,32]{0,2,1:T(8,128)(2,1)S(1)}, bf16[512,12,32]{0,2,1:T(8,128)(2,1)}, u32[]{:S(2)}) copy-start(bf16[512,12,32]{0,2,1:T(8,128)(2,1)} %get-tuple-element.181) | copy-start | bytes 1179652
  136.9 26.1 %copy-start.12 = (f32[512,12]{0,1:T(8,128)S(1)}, f32[512,12]{0,1:T(8,128)}, u32[]{:S(2)}) copy-start(f32[512,12]{0,1:T(8,128)} %copy-done.11) | copy-start | bytes 73732
  136.9 26.1 %copy-start.15 = (f32[512,12]{0,1:T(8,128)S(1)}, f32[512,12]{0,1:T(8,128)}, u32[]{:S(2)}) copy-start(f32[512,12]{0,1:T(8,128)} %copy-done.14) | copy-start | bytes 73732
  136.9 113.2 %all-gather.12.cloned.1.call-start = ((), (), s32[]{:S(2)}) async-start(), calls=%async_computation.2 | async-start | bytes 7077888 | tf_op jit(solution)/shard_map/all_gather | solution.py:148
  162.3 225.3 %all-gather.20.cloned.1.call-start = ((), (), s32[]{:S(2)}) async-start(), calls=%async_computation.6 | async-start | bytes 5308416 | tf_op jit(solution)/shard_map/all_gather | solution.py:179
  162.9 287.4 %all-gather.18.cloned.1.call-start = ((), (), s32[]{:S(2)}) async-start(), calls=%async_computation.5 | async-start | bytes 3932160 | tf_op jit(solution)/shard_map/all_gather | solution.py:174
  270.8 11.7 %copy-start = (f32[512,768]{0,1:T(8,128)S(1)}, f32[512,768]{0,1:T(8,128)}, u32[]{:S(2)}) copy-start(f32[512,768]{0,1:T(8,128)} %get-tuple-element.274) | copy-start | bytes 4718596 | tf_op jit(solution)/shard_map/while
  304.9 10.9 %copy-start = (f32[512,768]{0,1:T(8,128)S(1)}, f32[512,768]{0,1:T(8,128)}, u32[]{:S(2)}) copy-start(f32[512,768]{0,1:T(8,128)} %get-tuple-element.274) | copy-start | bytes 4718596 | tf_op jit(solution)/shard_map/while
  338.2 10.9 %copy-start = (f32[512,768]{0,1:T(8,128)S(1)}, f32[512,768]{0,1:T(8,128)}, u32[]{:S(2)}) copy-start(f32[512,768]{0,1:T(8,128)} %get-tuple-element.274) | copy-start | bytes 4718596 | tf_op jit(solution)/shard_map/while
  371.5 10.9 %copy-start = (f32[512,768]{0,1:T(8,128)S(1)}, f32[512,768]{0,1:T(8,128)}, u32[]{:S(2)}) copy-start(f32[512,768]{0,1:T(8,128)} %get-tuple-element.274) | copy-start | bytes 4718596 | tf_op jit(solution)/shard_map/while
  384.1 66.2 %copy-start.9 = (bf16[512,768]{1,0:T(8,128)(2,1)S(1)}, bf16[512,768]{1,0:T(8,128)(2,1)}, u32[]{:S(2)}) copy-start(bf16[512,768]{1,0:T(8,128)(2,1)} %param.12) | copy-start | bytes 2359300
  384.1 66.2 %copy-start.24 = (pred[512]{0:T(512)(128)(4,1)S(1)}, pred[512]{0:T(512)(128)(4,1)}, u32[]{:S(2)}) copy-start(pred[512]{0:T(512)(128)(4,1)} %subtract_compare_fusion) | copy-start | bytes 1540
  (21 other events, 23.7 us)
Sparse Core Ops, SparseCore 0:
  8.9 66.1 all-gather.7
  77.0 37.5 all-gather.13
  116.5 38.9 all-gather.9
  157.2 45.5 all-gather.15
  204.5 45.5 all-gather.11
  251.8 38.9 all-gather.19
  386.8 63.4 all-gather.17
